TPU v7x, 32 devices: a whole 2x2x4 slice. The times are simulated.
32 devices in a mesh: grp: 2 (over x), chol: 16 (over z, y, core).
Axes of the slice: x: 2, y: 2, z: 4, core: 2. Of those that a mesh axis runs over, the one named last changes fastest.
Arguments:
- chol_vectors: bfloat16 [2048, 32768], P(None, 'chol'), may hold values from -0.03125 to 0.03125
- mean_greens: bfloat16 [32768], P('chol'), may hold values from -6 to 6
- greens: bfloat16 [512, 32768], P(('grp', 'chol')), parts along dimension 0, may hold values from -6 to 6
- walker_order: int32 [512], P('grp'), parts along dimension 0, may hold values from 0 to 255, each once
- noise_field: float32 [512, 2048], P(('grp', 'chol')), parts along dimension 0, may hold values from -6 to 6
Outputs:
- shifted_field: float32 [512, 2048], P(('grp', 'chol')), parts along dimension 0
There are 2 independent parts, one for each index of `grp`. A program takes and returns all parts, laid end to end along the dimension named above; an argument that names none is the same for every part. Nothing has to cross between parts.
Inputs may be any that keep to these rules, and one draw needn't show every extreme that they name: `walker_order`: each row of greens appears once.
All inputs are finite; a program needn't handle non-finite values.
Results may differ from a plain program's by a relative error of at most 0.0012.
Values may be sent and summed in bfloat16 or wider, within the bound.
A program may use at most 64 MiB of HBM per device.

v0:
```python
import functools

import jax
import jax.numpy as jnp
from jax import lax
from jax.experimental import pallas as pl
from jax.experimental.pallas import tpu as pltpu
from jax.sharding import PartitionSpec as P

CHUNKS = 4
STEPS = 32000.0


def contract(left, right):
    return lax.dot_general(
        left, right, (((1,), (1,)), ((), ())), preferred_element_type=jnp.float32
    )


def encode(values):
    top = jnp.maximum(jnp.max(jnp.abs(values), axis=(0, 1), keepdims=True), 1e-30)
    return jnp.round(values * (STEPS / top)).astype(jnp.int32).astype(jnp.int16), top[0]


def decode(code, top):
    return code.astype(jnp.int32).astype(jnp.float32) * (top * (1.0 / STEPS))


def plain_per_device(chol_vectors, mean_greens, greens, walker_order, noise_field):
    pair_rows = lax.all_to_all(greens, "chol", split_axis=1, concat_axis=0, tiled=True)
    mean_part = jnp.dot(chol_vectors, mean_greens, preferred_element_type=jnp.float32)
    mean_field = lax.psum(mean_part, "chol")
    picked = jnp.take(pair_rows, walker_order, axis=0)
    raw_bias = lax.psum_scatter(
        contract(picked, chol_vectors), "chol", scatter_dimension=0, tiled=True
    )
    shift = jnp.tanh(raw_bias) - mean_field[None, :]
    return noise_field - shift


def kernel(
    outer, inner,
    order_hbm, mean_hbm, noise_hbm, chol_hbm, greens_hbm, out_ref,
    order_ref, mean_ref, noise_ref, chol, rows, part, core_in, y_out, y_code, y_top, y_in, y_top_in,
    z_out, z_code, z_top, z_in, z_top_in, mean_mine, mean_in,
    order_sem, mean_sem, noise_sem, chol_sem, own_sem, a2a_send, a2a_recv,
    core_send, core_recv, y_send, y_recv, y_top_send, y_top_recv,
    z_send, z_recv, z_top_send, z_top_recv, mean_send, mean_recv,
):
    cores = 2
    n = outer * inner * cores
    walkers, pairs = greens_hbm.shape[0], chol.shape[1]
    nchol = chol.shape[0]
    width = nchol // CHUNKS
    me = lax.axis_index("chol")
    c = me % cores
    y = (me // cores) % inner
    z = me // (cores * inner)

    def device(zz, yy, cc):
        return (zz * inner + yy) * cores + cc

    def remote(src, dst, send, recv, target):
        return pltpu.make_async_remote_copy(
            src_ref=src, dst_ref=dst, send_sem=send, recv_sem=recv,
            device_id={"chol": target}, device_id_type=pl.DeviceIdType.MESH,
        )

    offsets = [
        (dz, dy, dc)
        for dz in range(outer) for dy in range(inner) for dc in range(cores)
        if (dz, dy, dc) != (0, 0, 0)
    ]

    def shifted(dz, dy, dc):
        return device((z + dz) % outer, (y + dy) % inner, (c + dc) % cores)

    chol_copies = [
        pltpu.make_async_copy(
            chol_hbm.at[pl.ds(q * width, width), :], chol.at[pl.ds(q * width, width), :],
            chol_sem.at[q],
        )
        for q in range(CHUNKS)
    ]
    order_copy = pltpu.make_async_copy(order_hbm, order_ref, order_sem)
    mean_copy = pltpu.make_async_copy(mean_hbm, mean_ref, mean_sem)
    noise_copy = pltpu.make_async_copy(noise_hbm, noise_ref, noise_sem)
    own = pltpu.make_async_copy(
        greens_hbm.at[:, pl.ds(pl.multiple_of(me * pairs, pairs), pairs)], rows.at[me], own_sem
    )

    barrier = pltpu.get_barrier_semaphore()
    for offset in offsets:
        pl.semaphore_signal(
            barrier, inc=1, device_id={"chol": shifted(*offset)},
            device_id_type=pl.DeviceIdType.MESH,
        )
    for copy in [mean_copy, *chol_copies, own, order_copy, noise_copy]:
        copy.start()
    pl.semaphore_wait(barrier, n - 1)

    a2a = []
    for k, offset in enumerate(sorted(offsets, key=lambda o: (-o[0] * (outer - o[0]), -o[1], o[0]))):
        target = shifted(*offset)
        copy = remote(
            greens_hbm.at[:, pl.ds(pl.multiple_of(target * pairs, pairs), pairs)],
            rows.at[me], a2a_send.at[k], a2a_recv.at[k], target,
        )
        copy.start()
        a2a.append(copy)

    core_peer = shifted(0, 0, 1)
    y_peer = shifted(0, 1, 0)

    mean_copy.wait()
    mean_rows = jnp.broadcast_to(mean_ref[...].astype(jnp.float32).reshape(1, pairs), (16, pairs)).astype(jnp.bfloat16)
    for q in range(CHUNKS):
        chol_copies[q].wait()
        span = pl.ds(q * width, width)
        mean_mine[0, :, span] = contract(mean_rows, chol[span, :])[0:1, :]

    def mean_hop(at, stage, target):
        return remote(
            mean_mine.at[at], mean_in.at[stage], mean_send.at[stage], mean_recv.at[stage], target
        )

    core_hop = mean_hop(0, 0, core_peer)
    core_hop.start()

    own.wait()
    for copy in a2a:
        copy.wait()

    core_hop.wait()
    mean_mine[1] = mean_mine[0] + mean_in[0]
    y_hop = mean_hop(1, 1, y_peer)
    y_hop.start()

    order_copy.wait()
    source = lax.broadcasted_iota(jnp.int32, (n * walkers, n * walkers), 0)
    chosen = jnp.where(source == order_ref[...], 1.0, 0.0).astype(jnp.bfloat16)
    picked = lax.dot_general(
        chosen, rows[...].reshape(n * walkers, pairs), (((0,), (0,)), ((), ())),
        preferred_element_type=jnp.float32,
    ).astype(jnp.bfloat16)

    def core_copy(q):
        return remote(
            part.at[q, 1 - c], core_in.at[q], core_send.at[q], core_recv.at[q], core_peer
        )

    def y_copies(q):
        return (
            remote(y_code.at[q], y_in.at[q], y_send.at[q], y_recv.at[q], y_peer),
            remote(y_top.at[q], y_top_in.at[q], y_top_send.at[q], y_top_recv.at[q], y_peer),
        )

    def z_copies(q, dz):
        zz, at = (z + dz) % outer, dz - 1
        target = shifted(dz, 0, 0)
        return (
            remote(z_code.at[q, zz], z_in.at[q, at], z_send.at[q, at], z_recv.at[q, at], target),
            remote(
                z_top.at[q], z_top_in.at[q, at],
                z_top_send.at[q, at], z_top_recv.at[q, at], target,
            ),
        )

    def multiply(q):
        bias = contract(picked, chol[pl.ds(q * width, width), :])
        bias = bias.reshape(outer * inner, cores, walkers, width)
        for cc in range(cores):
            part[q, cc] = bias[:, cc]
        core_copy(q).start()

    def sum_cores(q):
        core_copy(q).wait()
        total = (part[q, c] + core_in[q]).reshape(outer, inner, walkers, width)
        for yy in range(inner):
            y_out[q, yy] = total[:, yy]
        y_code[q], y_top[q] = encode(y_out[q, 1 - y])
        for copy in y_copies(q):
            copy.start()

    def sum_inner(q):
        for copy in y_copies(q):
            copy.wait()
        total = y_out[q, y] + decode(y_in[q], y_top_in[q])
        z_out[q] = total
        z_code[q], z_top[q] = encode(total)
        for dz in range(1, outer):
            for copy in z_copies(q, dz):
                copy.start()

    def finish(q):
        for dz in range(1, outer):
            for copy in z_copies(q, dz):
                copy.wait()
        span = pl.ds(q * width, width)
        raw = z_out[q, z]
        for dz in range(1, outer):
            raw = raw + decode(z_in[q, dz - 1], z_top_in[q, dz - 1])
        out_ref[:, span] = noise_ref[:, span] - (jnp.tanh(raw) - mean_mine[3, :, span])

    for step in range(CHUNKS + 1):
        if step < CHUNKS:
            multiply(step)
        if step >= 1:
            sum_cores(step - 1)
    y_hop.wait()
    mean_mine[2] = mean_mine[1] + mean_in[1]
    hops = [mean_hop(2, 1 + dz, shifted(dz, 0, 0)) for dz in range(1, outer)]
    for hop in hops:
        hop.start()
    for q in range(CHUNKS):
        sum_inner(q)
    for hop in hops:
        hop.wait()
    total = mean_mine[2]
    for dz in range(1, outer):
        total = total + mean_in[1 + dz]
    mean_mine[3] = total
    noise_copy.wait()
    for q in range(CHUNKS):
        finish(q)


def fused_per_device(outer, inner, chol_vectors, mean_greens, greens, walker_order, noise_field):
    nchol, pairs = chol_vectors.shape
    walkers = greens.shape[0]
    n = outer * inner * 2
    width = nchol // CHUNKS
    vmem = pl.BlockSpec(memory_space=pltpu.VMEM)
    hbm = pl.BlockSpec(memory_space=pltpu.HBM)
    dma = pltpu.SemaphoreType.DMA
    f32, i16 = jnp.float32, jnp.int16
    return pl.pallas_call(
        functools.partial(kernel, outer, inner),
        out_shape=pltpu.VMEM(noise_field.shape, f32),
        in_specs=[hbm] * 5,
        out_specs=vmem,
        scratch_shapes=[
            pltpu.VMEM((1, n * walkers), jnp.int32),
            pltpu.VMEM((pairs,), jnp.bfloat16),
            pltpu.VMEM(noise_field.shape, f32),
            pltpu.VMEM((nchol, pairs), jnp.bfloat16),
            pltpu.VMEM((n, walkers, pairs), jnp.bfloat16),
            pltpu.VMEM((CHUNKS, 2, outer * inner, walkers, width), f32),
            pltpu.VMEM((CHUNKS, outer * inner, walkers, width), f32),
            pltpu.VMEM((CHUNKS, inner, outer, walkers, width), f32),
            pltpu.VMEM((CHUNKS, outer, walkers, width), i16),
            pltpu.VMEM((CHUNKS, 1, width), f32),
            pltpu.VMEM((CHUNKS, outer, walkers, width), i16),
            pltpu.VMEM((CHUNKS, 1, width), f32),
            pltpu.VMEM((CHUNKS, outer, walkers, width), f32),
            pltpu.VMEM((CHUNKS, outer, walkers, width), i16),
            pltpu.VMEM((CHUNKS, 1, width), f32),
            pltpu.VMEM((CHUNKS, outer - 1, walkers, width), i16),
            pltpu.VMEM((CHUNKS, outer - 1, 1, width), f32),
            pltpu.VMEM((4, 1, nchol), f32),
            pltpu.VMEM((1 + outer, 1, nchol), f32),
            dma, dma, dma, dma((CHUNKS,)), dma, dma((n - 1,)), dma((n - 1,)),
            dma((CHUNKS,)), dma((CHUNKS,)),
            dma((CHUNKS,)), dma((CHUNKS,)), dma((CHUNKS,)), dma((CHUNKS,)),
            dma((CHUNKS, outer - 1)), dma((CHUNKS, outer - 1)),
            dma((CHUNKS, outer - 1)), dma((CHUNKS, outer - 1)),
            dma((1 + outer,)), dma((1 + outer,)),
        ],
        compiler_params=pltpu.CompilerParams(
            collective_id=0, has_side_effects=True, vmem_limit_bytes=60 * 1024 * 1024
        ),
    )(walker_order[None, :], mean_greens, noise_field, chol_vectors, greens)


def solution(mesh):
    placed = (
        P(None, "chol"),
        P("chol"),
        P(("grp", "chol"), None),
        P("grp"),
        P(("grp", "chol"), None),
    )
    chips = mesh.shape["chol"] // 2
    inner = 1
    while (2 * inner) ** 2 <= chips:
        inner *= 2
    outer = chips // inner
    body = functools.partial(fused_per_device, outer, inner) if inner == 2 else plain_per_device
    return jax.shard_map(
        body, mesh=mesh, in_specs=placed, out_specs=P(("grp", "chol"), None), check_vma=False
    )
```

profile of v0, /device:TPU:0, one launch (start us, length us, event | category | flops | bytes accessed | tf_op | source)
XLA Modules:
  0.0 44.6 jit_solution(8975184348431359708)
XLA Ops:
  0.0 43.9 %shard_map.55 = f32[16,2048]{1,0:T(8,128)S(1)} custom-call(s32[1,256]{1,0:T(1,128)} %bitcast.1, bf16[2048]{0:T(1024)(128)(2,1)} %mean_hbm.1, f32[16,2048]{1,0:T(8,128)} %noise_hbm.1, bf16[2048,2048]{1,0:T(8,128)(2,1)} %chol_hbm.1, bf16[16,32768]{1,0:T(8,128)(2,1)} %greens_hbm.1), custom_call_target="tpu_custom_call" | custom-call | tf_op jit(solution)/shard_map/pallas_call | solution.py:237
  43.9 0.7 %copy.7 = f32[16,2048]{1,0:T(8,128)} copy(f32[16,2048]{1,0:T(8,128)S(1)} %shard_map.55) | data formatting | bytes 262144
where the time goes:
time: 44.7 us; the launch traced here: 44.6 us
  Pallas kernels  43.9 us (98%)
  local copies, waits for them, and re-layouts  0.66 us (1%)
    pallas_call x1, Pallas kernels, fused_per_device(): pl.pallas_call(functools.partial(kernel, outer, inner), out_shape=pltpu.V...  43.9 us

commit v1 on v0

v1 whole, which is shorter than its diff:
```python
import functools

import jax
import jax.numpy as jnp
from jax import lax
from jax.experimental import pallas as pl
from jax.experimental.pallas import tpu as pltpu
from jax.sharding import PartitionSpec as P

CHUNKS = 4
LAST = 2
STEPS = 32000.0


def contract(left, right):
    return lax.dot_general(
        left, right, (((1,), (1,)), ((), ())), preferred_element_type=jnp.float32
    )


def encode(values):
    top = jnp.maximum(jnp.max(jnp.abs(values), axis=(0, 1), keepdims=True), 1e-30)
    return jnp.round(values * (STEPS / top)).astype(jnp.int32).astype(jnp.int16), top[0]


def decode(code, top):
    return code.astype(jnp.int32).astype(jnp.float32) * (top * (1.0 / STEPS))


def plain_per_device(chol_vectors, mean_greens, greens, walker_order, noise_field):
    pair_rows = lax.all_to_all(greens, "chol", split_axis=1, concat_axis=0, tiled=True)
    mean_part = jnp.dot(chol_vectors, mean_greens, preferred_element_type=jnp.float32)
    mean_field = lax.psum(mean_part, "chol")
    picked = jnp.take(pair_rows, walker_order, axis=0)
    raw_bias = lax.psum_scatter(
        contract(picked, chol_vectors), "chol", scatter_dimension=0, tiled=True
    )
    shift = jnp.tanh(raw_bias) - mean_field[None, :]
    return noise_field - shift


def order_key(mine, target, stage, r, dy, dc, p):
    to_middle = 0 < target[0] < 3
    cross = abs(r) >= 2 and not to_middle
    filler = (mine[0] == 0 and target[0] == 1) or (mine[0] == 1 and target == (2, mine[1]) and p == 0 and dc == 0)
    if not cross and not filler:
        stage = 99
    return (stage, p, -abs(r), -dy, dc, p)


def kernel(
    outer, inner,
    order_hbm, mean_hbm, noise_hbm, chol_hbm, greens_hbm, out_ref,
    order_ref, mean_ref, noise_ref, chol, rows_first, rows_last, chosen, part, core_in, y_out, y_code, y_top, y_in, y_top_in,
    z_out, z_code, z_top, z_in, z_top_in, mean_mine, mean_in,
    order_sem, mean_sem, noise_sem, chol_sem, own_sem, near_sem, a2a_send, a2a_recv,
    core_send, core_recv, y_send, y_recv, z_send, z_recv, mean_send, mean_recv,
):
    cores = 2
    n = outer * inner * cores
    walkers, pairs = greens_hbm.shape[0], chol.shape[1]
    nchol = chol.shape[0]
    width = nchol // CHUNKS
    rows = (rows_first, rows_last)
    starts = (0, rows_first.shape[2])
    me = lax.axis_index("chol")
    c = me % cores
    y = (me // cores) % inner
    z = me // (cores * inner)
    def device(zz, yy, cc):
        return (zz * inner + yy) * cores + cc

    def remote(src, dst, send, recv, target):
        return pltpu.make_async_remote_copy(
            src_ref=src, dst_ref=dst, send_sem=send, recv_sem=recv,
            device_id={"chol": target}, device_id_type=pl.DeviceIdType.MESH,
        )

    offsets = [
        (dz, dy, dc)
        for dz in range(outer) for dy in range(inner) for dc in range(cores)
        if (dz, dy, dc) != (0, 0, 0)
    ]

    def shifted(dz, dy, dc):
        return device((z + dz) % outer, (y + dy) % inner, (c + dc) % cores)

    core_peer = shifted(0, 0, 1)
    y_peer = shifted(0, 1, 0)

    def signal(sem, target):
        pl.semaphore_signal(
            sem, inc=1, device_id={"chol": target}, device_id_type=pl.DeviceIdType.MESH
        )

    barrier = pltpu.get_barrier_semaphore()
    chips = [(zz, yy) for zz in range(outer) for yy in range(inner)]

    @pl.when(c == 0)
    def _():
        signal(barrier, core_peer)

    for zz, yy in reversed(chips):
        @pl.when((zz >= z) & (yy >= y) & ((zz > z) | (yy > y)))
        def _():
            for cc in range(cores):
                signal(barrier, device(zz, yy, cc))

    chol_copy = pltpu.make_async_copy(chol_hbm, chol, chol_sem)
    order_copy = pltpu.make_async_copy(order_hbm, order_ref, order_sem)
    mean_copy = pltpu.make_async_copy(mean_hbm, mean_ref, mean_sem)
    noise_copy = pltpu.make_async_copy(noise_hbm, noise_ref, noise_sem)

    def span_of(owner, p):
        size = rows[p].shape[2]
        return pl.ds(pl.multiple_of(owner * pairs + starts[p], 128), size)

    own = [
        pltpu.make_async_copy(greens_hbm.at[:, span_of(me, p)], rows[p].at[me], own_sem.at[p])
        for p in range(2)
    ]
    a2a = []
    for p in range(2):
        a2a.append([])
        for k, offset in enumerate(offsets):
            target = shifted(*offset)
            a2a[p].append(remote(
                greens_hbm.at[:, span_of(target, p)], rows[p].at[me],
                a2a_send.at[p, k], a2a_recv.at[p, k], target,
            ))

    for copy in [order_copy, mean_copy, chol_copy, *own, noise_copy]:
        copy.start()
    below_here = cores * ((z + 1) * (y + 1) - 1) + c

    @pl.when(below_here > 0)
    def _():
        pl.semaphore_wait(barrier, below_here)

    here = z * inner + y

    @pl.when(c == cores - 1)
    def _():
        signal(near_sem.at[here], core_peer)
        for zz, yy in chips:
            @pl.when((zz <= z) & (yy <= y) & ((zz < z) | (yy < y)))
            def _():
                for cc in range(cores):
                    signal(near_sem.at[here], device(zz, yy, cc))

    for zv, yv in chips:
        far = 1 if zv < outer // 2 else -1
        above = [(zz, yy) for zz, yy in chips if zz >= zv and yy >= yv and (zz, yy) != (zv, yv)]
        below = {(zz, yy) for zz, yy in chips if zz <= zv and yy <= yv}
        waits, todo, left_over = [None, (zv, yv), *sorted(above, key=lambda a: (sum(a), a))], [], []
        known = below - {(zv, yv)}
        stage_of = {chip: 0 for chip in known}
        for stage, chip in enumerate(waits):
            if chip is not None:
                for zz, yy in chips:
                    if zz <= chip[0] and yy <= chip[1]:
                        stage_of.setdefault((zz, yy), stage)
        for p in range(2):
            for k, (dz, dy, dc) in enumerate(offsets):
                target = (zv + dz) % outer, (yv + dy) % inner
                r = (target[0] - zv) * far
                stage, *key = order_key((zv, yv), target, stage_of[target], r, dy, dc, p)
                todo.append((stage, key, p, k))
        todo.sort()

        @pl.when((z == zv) & (y == yv))
        def _():
            for stage, chip in enumerate(waits):
                if chip == (zv, yv):
                    @pl.when(c == 0)
                    def _():
                        pl.semaphore_wait(near_sem.at[zv * inner + yv], 1)
                elif chip is not None:
                    pl.semaphore_wait(near_sem.at[chip[0] * inner + chip[1]], 1)
                for when, _, p, k in todo:
                    if when == stage or (when > stage and stage == len(waits) - 1):
                        a2a[p][k].start()

    order_copy.wait()
    source = lax.broadcasted_iota(jnp.int32, (n * walkers, n * walkers), 0)
    chosen[...] = jnp.where(source == order_ref[...], 1.0, 0.0).T.astype(jnp.bfloat16)

    mean_copy.wait()
    chol_copy.wait()
    mean_rows = jnp.broadcast_to(mean_ref[...].astype(jnp.float32).reshape(1, pairs), (16, pairs)).astype(jnp.bfloat16)
    for q in range(CHUNKS):
        span = pl.ds(q * width, width)
        mean_mine[0, :, span] = contract(mean_rows, chol[span, :])[0:1, :]

    def mean_hop(at, stage, target):
        return remote(
            mean_mine.at[at], mean_in.at[stage], mean_send.at[stage], mean_recv.at[stage], target
        )

    core_hop = mean_hop(0, 0, core_peer)
    y_hop = mean_hop(1, 1, y_peer)
    z_hops = [mean_hop(2, 1 + dz, shifted(dz, 0, 0)) for dz in range(1, outer)]
    core_hop.start()
    core_hop.wait()
    mean_mine[1] = mean_mine[0] + mean_in[0]
    y_hop.start()

    def pick(p):
        own[p].wait()
        for copy in a2a[p]:
            copy.wait_recv()
        size = rows[p].shape[2]
        return jnp.dot(
            chosen[...], rows[p][...].reshape(n * walkers, size), preferred_element_type=jnp.float32
        ).astype(jnp.bfloat16)

    def add(p, picked, q):
        size = rows[p].shape[2]
        bias = contract(picked, chol[pl.ds(q * width, width), pl.ds(starts[p], size)])
        bias = bias.reshape(outer * inner, cores, walkers, width)
        for cc in range(cores):
            part[q, cc] = bias[:, cc] if p == 0 else part[q, cc] + bias[:, cc]

    picked = pick(0)
    for q in range(CHUNKS):
        add(0, picked, q)
    y_hop.wait()
    mean_mine[2] = mean_mine[1] + mean_in[1]
    for hop in z_hops:
        hop.start()
    picked = pick(1)

    def core_copy(q):
        return remote(
            part.at[q, 1 - c], core_in.at[q], core_send.at[q], core_recv.at[q], core_peer
        )

    half = outer // 2

    def y_copies(q, h):
        return (
            remote(y_code.at[q, h], y_in.at[q, h], y_send.at[q, h, 0], y_recv.at[q, h, 0], y_peer),
            remote(y_top.at[q, h], y_top_in.at[q, h], y_send.at[q, h, 1], y_recv.at[q, h, 1], y_peer),
        )

    def z_copies(q, h, at, slot, zz, target):
        return (
            remote(z_code.at[q, h, at], z_in.at[q, slot], z_send.at[q, zz, 0], z_recv.at[q, slot, 0], target),
            remote(z_top.at[q, h], z_top_in.at[q, slot], z_send.at[q, zz, 1], z_recv.at[q, slot, 1], target),
        )

    def send_y(q, h):
        y_code[q, h], y_top[q, h] = encode(y_out[q, 1 - y, half * h:half * (h + 1)])
        for copy in y_copies(q, h):
            copy.start()

    def sum_cores(q):
        core_copy(q).wait()
        total = (part[q, c] + core_in[q]).reshape(outer, inner, walkers, width)
        for yy in range(inner):
            y_out[q, yy] = total[:, yy]
        send_y(q, 0)

    def sum_inner(q, h):
        for copy in y_copies(q, h):
            copy.wait()
        total = y_out[q, y, half * h:half * (h + 1)] + decode(y_in[q, h], y_top_in[q, h])
        z_out[q, half * h:half * (h + 1)] = total
        z_code[q, h], z_top[q, h] = encode(total)
        for at in range(half):
            zz = half * h + at

            @pl.when(z != zz)
            def _():
                for copy in z_copies(q, h, at, z, zz, device(zz, y, c)):
                    copy.start()

    def finish(q):
        span = pl.ds(q * width, width)
        raw = z_out[q, z]
        for dz in range(1, outer):
            zz = (z + dz) % outer
            for copy in z_copies(q, 0, 0, zz, zz, device(zz, y, c)):
                copy.wait_recv()
            raw = raw + decode(z_in[q, zz], z_top_in[q, zz])
        out_ref[:, span] = noise_ref[:, span] - (jnp.tanh(raw) - mean_mine[3, :, span])

    for step in range(CHUNKS + 1):
        if step < CHUNKS:
            add(1, picked, step)
            core_copy(step).start()
        if step >= 1:
            sum_cores(step - 1)
    for q in range(CHUNKS):
        send_y(q, 1)
    for h in range(2):
        for q in range(CHUNKS):
            sum_inner(q, h)
    noise_copy.wait()
    for hop in z_hops:
        hop.wait()
    mean = mean_mine[2]
    for dz in range(1, outer):
        mean = mean + mean_in[1 + dz]
    mean_mine[3] = mean
    for q in range(CHUNKS):
        finish(q)
    for q in range(CHUNKS):
        for dz in range(1, outer):
            zz = (z + dz) % outer
            for copy in z_copies(q, 0, 0, zz, zz, device(zz, y, c)):
                copy.wait_send()
    for p in range(2):
        for copy in a2a[p]:
            copy.wait_send()


def fused_per_device(outer, inner, chol_vectors, mean_greens, greens, walker_order, noise_field):
    nchol, pairs = chol_vectors.shape
    walkers = greens.shape[0]
    n = outer * inner * 2
    width = nchol // CHUNKS
    last = pairs // LAST
    halves = (CHUNKS, 2, outer // 2, walkers, width)
    vmem = pl.BlockSpec(memory_space=pltpu.VMEM)
    hbm = pl.BlockSpec(memory_space=pltpu.HBM)
    dma = pltpu.SemaphoreType.DMA
    f32, i16 = jnp.float32, jnp.int16
    return pl.pallas_call(
        functools.partial(kernel, outer, inner),
        out_shape=pltpu.VMEM(noise_field.shape, f32),
        in_specs=[hbm] * 5,
        out_specs=vmem,
        scratch_shapes=[
            pltpu.VMEM((1, n * walkers), jnp.int32),
            pltpu.VMEM((pairs,), jnp.bfloat16),
            pltpu.VMEM(noise_field.shape, f32),
            pltpu.VMEM((nchol, pairs), jnp.bfloat16),
            pltpu.VMEM((n, walkers, pairs - last), jnp.bfloat16),
            pltpu.VMEM((n, walkers, last), jnp.bfloat16),
            pltpu.VMEM((n * walkers, n * walkers), jnp.bfloat16),
            pltpu.VMEM((CHUNKS, 2, outer * inner, walkers, width), f32),
            pltpu.VMEM((CHUNKS, outer * inner, walkers, width), f32),
            pltpu.VMEM((CHUNKS, inner, outer, walkers, width), f32),
            *[pltpu.VMEM(halves, i16), pltpu.VMEM((CHUNKS, 2, 1, width), f32)] * 2,
            pltpu.VMEM((CHUNKS, outer, walkers, width), f32),
            pltpu.VMEM(halves, i16), pltpu.VMEM((CHUNKS, 2, 1, width), f32),
            pltpu.VMEM((CHUNKS, outer, walkers, width), i16), pltpu.VMEM((CHUNKS, outer, 1, width), f32),
            pltpu.VMEM((4, 1, nchol), f32),
            pltpu.VMEM((1 + outer, 1, nchol), f32),
            dma, dma, dma, dma, dma((2,)), pltpu.SemaphoreType.REGULAR((outer * inner,)),
            dma((2, n - 1)), dma((2, n - 1)),
            dma((CHUNKS,)), dma((CHUNKS,)), dma((CHUNKS, 2, 2)), dma((CHUNKS, 2, 2)),
            dma((CHUNKS, outer, 2)), dma((CHUNKS, outer, 2)),
            dma((1 + outer,)), dma((1 + outer,)),
        ],
        compiler_params=pltpu.CompilerParams(
            collective_id=0, has_side_effects=True, vmem_limit_bytes=60 * 1024 * 1024
        ),
    )(walker_order[None, :], mean_greens, noise_field, chol_vectors, greens)


def solution(mesh):
    placed = (
        P(None, "chol"),
        P("chol"),
        P(("grp", "chol"), None),
        P("grp"),
        P(("grp", "chol"), None),
    )
    chips = mesh.shape["chol"] // 2
    inner = 1
    while (2 * inner) ** 2 <= chips:
        inner *= 2
    outer = chips // inner
    body = functools.partial(fused_per_device, outer, inner) if (outer, inner) == (4, 2) else plain_per_device
    return jax.shard_map(
        body, mesh=mesh, in_specs=placed, out_specs=P(("grp", "chol"), None), check_vma=False
    )
```

time: 44.7 us -> 43 us (0.962)
  Pallas kernels: 43.9 us -> 42.1 us
    pallas_call x1, Pallas kernels: 43.9 us -> 42.1 us  [fused_per_device(): pl.pallas_call(functools.partial(kernel, outer, inner), out_shape=pltpu.V...]
where the time goes in v1:
time: 43 us; the launch traced here: 42.8 us
  Pallas kernels  42.1 us (98%)
  local copies, waits for them, and re-layouts  0.66 us (2%)
    pallas_call x1, Pallas kernels, fused_per_device(): pl.pallas_call(functools.partial(kernel, outer, inner), out_shape=pltpu.V...  42.1 us

profile of v1, /device:TPU:0, one launch (start us, length us, event | category | flops | bytes accessed | tf_op | source)
XLA Modules:
  0.0 42.8 jit_solution(7619465296316773567)
XLA Ops:
  0.0 42.1 %shard_map.55 = f32[16,2048]{1,0:T(8,128)S(1)} custom-call(s32[1,256]{1,0:T(1,128)} %bitcast.1, bf16[2048]{0:T(1024)(128)(2,1)} %mean_hbm.1, f32[16,2048]{1,0:T(8,128)} %noise_hbm.1, bf16[2048,2048]{1,0:T(8,128)(2,1)} %chol_hbm.1, bf16[16,32768]{1,0:T(8,128)(2,1)} %greens_hbm.1), custom_call_target="tpu_custom_call" | custom-call | tf_op jit(solution)/shard_map/pallas_call | solution.py:329
  42.2 0.7 %copy.7 = f32[16,2048]{1,0:T(8,128)} copy(f32[16,2048]{1,0:T(8,128)S(1)} %shard_map.55) | data formatting | bytes 262144

commit v2 on v1

--- a/solution.py
+++ b/solution.py
@@ -42,16 +42,16 @@
 def order_key(mine, target, stage, r, dy, dc, p):
     to_middle = 0 < target[0] < 3
     cross = abs(r) >= 2 and not to_middle
-    filler = (mine[0] == 0 and target[0] == 1) or (mine[0] == 1 and target == (2, mine[1]) and p == 0 and dc == 0)
+    filler = (mine[0] == 0 and target[0] == 1) or (mine[0] == 1 and target == (2, mine[1]) and p == 0)
     if not cross and not filler:
         stage = 99
-    return (stage, p, -abs(r), -dy, dc, p)
+    return (stage, p, -abs(r), -dy, dc)
 
 
 def kernel(
     outer, inner,
     order_hbm, mean_hbm, noise_hbm, chol_hbm, greens_hbm, out_ref,
-    order_ref, mean_ref, noise_ref, chol, rows_first, rows_last, chosen, part, core_in, y_out, y_code, y_top, y_in, y_top_in,
+    order_ref, mean_ref, noise_ref, chol, rows_first, rows_last, chosen, part, core_in, y_code, y_top, y_in, y_top_in,
     z_out, z_code, z_top, z_in, z_top_in, mean_mine, mean_in,
     order_sem, mean_sem, noise_sem, chol_sem, own_sem, near_sem, a2a_send, a2a_recv,
     core_send, core_recv, y_send, y_recv, z_send, z_recv, mean_send, mean_recv,
@@ -217,9 +217,9 @@
     def add(p, picked, q):
         size = rows[p].shape[2]
         bias = contract(picked, chol[pl.ds(q * width, width), pl.ds(starts[p], size)])
-        bias = bias.reshape(outer * inner, cores, walkers, width)
+        bias = bias.reshape(outer, inner, cores, walkers, width)
         for cc in range(cores):
-            part[q, cc] = bias[:, cc] if p == 0 else part[q, cc] + bias[:, cc]
+            part[q, cc] = bias[:, :, cc] if p == 0 else part[q, cc] + bias[:, :, cc]
 
     picked = pick(0)
     for q in range(CHUNKS):
@@ -249,22 +249,23 @@
             remote(z_top.at[q, h], z_top_in.at[q, slot], z_send.at[q, zz, 1], z_recv.at[q, slot, 1], target),
         )
 
+    def both_cores(q, h, yy):
+        z_part = pl.ds(half * h, half)
+        return part[q, c, z_part, yy] + core_in[q, z_part, yy]
+
     def send_y(q, h):
-        y_code[q, h], y_top[q, h] = encode(y_out[q, 1 - y, half * h:half * (h + 1)])
+        y_code[q, h], y_top[q, h] = encode(both_cores(q, h, 1 - y))
         for copy in y_copies(q, h):
             copy.start()
 
     def sum_cores(q):
         core_copy(q).wait()
-        total = (part[q, c] + core_in[q]).reshape(outer, inner, walkers, width)
-        for yy in range(inner):
-            y_out[q, yy] = total[:, yy]
         send_y(q, 0)
 
     def sum_inner(q, h):
         for copy in y_copies(q, h):
             copy.wait()
-        total = y_out[q, y, half * h:half * (h + 1)] + decode(y_in[q, h], y_top_in[q, h])
+        total = both_cores(q, h, y) + decode(y_in[q, h], y_top_in[q, h])
         z_out[q, half * h:half * (h + 1)] = total
         z_code[q, h], z_top[q, h] = encode(total)
         for at in range(half):
@@ -285,12 +286,12 @@
             raw = raw + decode(z_in[q, zz], z_top_in[q, zz])
         out_ref[:, span] = noise_ref[:, span] - (jnp.tanh(raw) - mean_mine[3, :, span])
 
-    for step in range(CHUNKS + 1):
+    for step in range(CHUNKS + 2):
         if step < CHUNKS:
             add(1, picked, step)
             core_copy(step).start()
-        if step >= 1:
-            sum_cores(step - 1)
+        if step >= 2:
+            sum_cores(step - 2)
     for q in range(CHUNKS):
         send_y(q, 1)
     for h in range(2):
@@ -339,9 +340,8 @@
             pltpu.VMEM((n, walkers, pairs - last), jnp.bfloat16),
             pltpu.VMEM((n, walkers, last), jnp.bfloat16),
             pltpu.VMEM((n * walkers, n * walkers), jnp.bfloat16),
-            pltpu.VMEM((CHUNKS, 2, outer * inner, walkers, width), f32),
-            pltpu.VMEM((CHUNKS, outer * inner, walkers, width), f32),
-            pltpu.VMEM((CHUNKS, inner, outer, walkers, width), f32),
+            pltpu.VMEM((CHUNKS, 2, outer, inner, walkers, width), f32),
+            pltpu.VMEM((CHUNKS, outer, inner, walkers, width), f32),
             *[pltpu.VMEM(halves, i16), pltpu.VMEM((CHUNKS, 2, 1, width), f32)] * 2,
             pltpu.VMEM((CHUNKS, outer, walkers, width), f32),
             pltpu.VMEM(halves, i16), pltpu.VMEM((CHUNKS, 2, 1, width), f32),

time: 43 us -> 42.4 us (0.986)
  Pallas kernels: 42.1 us -> 41.6 us
    pallas_call x1, Pallas kernels: 42.1 us -> 41.6 us  [fused_per_device(): pl.pallas_call(functools.partial(kernel, outer, inner), out_shape=pltpu.V...]
where the time goes in v2:
time: 42.4 us; the launch traced here: 42.3 us
  Pallas kernels  41.6 us (98%)
  local copies, waits for them, and re-layouts  0.66 us (2%)
    pallas_call x1, Pallas kernels, fused_per_device(): pl.pallas_call(functools.partial(kernel, outer, inner), out_shape=pltpu.V...  41.6 us

profile of v2, /device:TPU:0, one launch (start us, length us, event | category | flops | bytes accessed | tf_op | source)
XLA Modules:
  0.0 42.3 jit_solution(9995388263756303721)
XLA Ops:
  0.0 41.6 %shard_map.55 = f32[16,2048]{1,0:T(8,128)S(1)} custom-call(s32[1,256]{1,0:T(1,128)} %bitcast.1, bf16[2048]{0:T(1024)(128)(2,1)} %mean_hbm.1, f32[16,2048]{1,0:T(8,128)} %noise_hbm.1, bf16[2048,2048]{1,0:T(8,128)(2,1)} %chol_hbm.1, bf16[16,32768]{1,0:T(8,128)(2,1)} %greens_hbm.1), custom_call_target="tpu_custom_call" | custom-call | tf_op jit(solution)/shard_map/pallas_call | solution.py:330
  41.6 0.7 %copy.7 = f32[16,2048]{1,0:T(8,128)} copy(f32[16,2048]{1,0:T(8,128)S(1)} %shard_map.55) | data formatting | bytes 262144

commit v3 on v2

--- a/solution.py
+++ b/solution.py
@@ -230,12 +230,14 @@
         hop.start()
     picked = pick(1)
 
-    def core_copy(q):
+    half = outer // 2
+
+    def core_copy(q, h):
+        chips_of = pl.ds(h * half, half)
         return remote(
-            part.at[q, 1 - c], core_in.at[q], core_send.at[q], core_recv.at[q], core_peer
-        )
-
-    half = outer // 2
+            part.at[q, 1 - c, chips_of], core_in.at[q, chips_of],
+            core_send.at[q, h], core_recv.at[q, h], core_peer,
+        )
 
     def y_copies(q, h):
         return (
@@ -259,8 +261,11 @@
             copy.start()
 
     def sum_cores(q):
-        core_copy(q).wait()
-        send_y(q, 0)
+        sum_half(q, 0)
+
+    def sum_half(q, h):
+        core_copy(q, h).wait()
+        send_y(q, h)
 
     def sum_inner(q, h):
         for copy in y_copies(q, h):
@@ -289,11 +294,14 @@
     for step in range(CHUNKS + 2):
         if step < CHUNKS:
             add(1, picked, step)
-            core_copy(step).start()
+            core_copy(step, 0).start()
         if step >= 2:
             sum_cores(step - 2)
-    for q in range(CHUNKS):
-        send_y(q, 1)
+        if step == CHUNKS - 1:
+            for q in range(CHUNKS):
+                core_copy(q, 1).start()
+    for q in range(CHUNKS):
+        sum_half(q, 1)
     for h in range(2):
         for q in range(CHUNKS):
             sum_inner(q, h)
@@ -350,7 +358,7 @@
             pltpu.VMEM((1 + outer, 1, nchol), f32),
             dma, dma, dma, dma, dma((2,)), pltpu.SemaphoreType.REGULAR((outer * inner,)),
             dma((2, n - 1)), dma((2, n - 1)),
-            dma((CHUNKS,)), dma((CHUNKS,)), dma((CHUNKS, 2, 2)), dma((CHUNKS, 2, 2)),
+            dma((CHUNKS, 2)), dma((CHUNKS, 2)), dma((CHUNKS, 2, 2)), dma((CHUNKS, 2, 2)),
             dma((CHUNKS, outer, 2)), dma((CHUNKS, outer, 2)),
             dma((1 + outer,)), dma((1 + outer,)),
         ],

time: 42.4 us -> 42.3 us (level)
  no operation moved by 1% of the time
where the time goes in v3:
time: 42.3 us; the launch traced here: 42.2 us
  Pallas kernels  41.5 us (98%)
  local copies, waits for them, and re-layouts  0.66 us (2%)
    pallas_call x1, Pallas kernels, fused_per_device(): pl.pallas_call(functools.partial(kernel, outer, inner), out_shape=pltpu.V...  41.5 us

profile of v3, /device:TPU:0, one launch (start us, length us, event | category | flops | bytes accessed | tf_op | source)
XLA Modules:
  0.0 42.2 jit_solution(6225731602049856044)
XLA Ops:
  0.0 41.5 %shard_map.55 = f32[16,2048]{1,0:T(8,128)S(1)} custom-call(s32[1,256]{1,0:T(1,128)} %bitcast.1, bf16[2048]{0:T(1024)(128)(2,1)} %mean_hbm.1, f32[16,2048]{1,0:T(8,128)} %noise_hbm.1, bf16[2048,2048]{1,0:T(8,128)(2,1)} %chol_hbm.1, bf16[16,32768]{1,0:T(8,128)(2,1)} %greens_hbm.1), custom_call_target="tpu_custom_call" | custom-call | tf_op jit(solution)/shard_map/pallas_call | solution.py:338
  41.5 0.7 %copy.7 = f32[16,2048]{1,0:T(8,128)} copy(f32[16,2048]{1,0:T(8,128)S(1)} %shard_map.55) | data formatting | bytes 262144
